TPU v7x, 32 devices: a whole 2x2x4 slice. The times are simulated.
32 devices in a mesh: req: 4 (over z), head: 2 (over core), exp: 4 (over y, x).
Axes of the slice: x: 2, y: 2, z: 4, core: 2. Of those that a mesh axis runs over, the one named last changes fastest.
Arguments:
- queries: bfloat16 [64, 64, 128], P(('req', 'exp'), 'head'), may hold values from -18 to 18
- keys: bfloat16 [64, 512, 4, 128], P(('req', 'exp'), None, 'head'), may hold values from -15 to 15
- values: bfloat16 [64, 512, 4, 128], P(('req', 'exp'), None, 'head'), may hold values from -12 to 12
- lengths: int32 [64], P(('req', 'exp')), may hold values from 1 to 512, as said below
- out_weight: bfloat16 [8192, 4096], P('head', 'exp'), may hold values from -0.0625 to 0.0625
- resid: bfloat16 [64, 4096], P('req', 'exp'), may hold values from -11 to 11
- norm_gain: float32 [4096], replicated, may hold values from 0.25 to 1.75
- expert_ids: int32 [64, 8], P('req'), may hold values from 0 to 15, all different within a row; in each aligned block of 16 rows (0 to 15, 16 to 31, ...) at most 8 rows name the same one
- route_weights: float32 [64, 8], P('req'), may hold values from 0.1 to 1
- w_gate: bfloat16 [16, 4096, 768], P(('req', 'exp'), None, 'head'), may hold values from -0.09375 to 0.09375
- w_up: bfloat16 [16, 4096, 768], P(('req', 'exp'), None, 'head'), may hold values from -0.09375 to 0.09375
- w_down: bfloat16 [16, 768, 4096], P(('req', 'exp'), 'head'), may hold values from -0.21875 to 0.21875
Outputs:
- layer_out: bfloat16 [64, 4096], P('req', 'exp')
Inputs may be any that keep to these rules, and one draw needn't show every extreme that they name: `expert_ids`: within each aligned block of 16 rows (the tokens of one index of req), a row names 8 different experts and no expert is named by more than 8 rows; some expert is named by exactly 8 rows. `lengths`: some question's cache is full.
All inputs are finite; a program needn't handle non-finite values.
Results may differ from a plain program's by a relative error of at most 0.0049.
Values may be sent and summed in bfloat16 or wider, within the bound.
No kernel may reach another device: no remote copies, remote signals or barrier semaphores. Data moves between devices by JAX's collectives and lax.ppermute only.
A program may use at most 64 MiB of HBM per device.

v0:
```python
import math
import jax
import jax.numpy as jnp
from jax import lax
from jax.sharding import PartitionSpec as P


def local(
    queries,
    keys,
    values,
    lengths,
    out_weight,
    resid,
    norm_gain,
    expert_ids,
    route_weights,
    w_gate,
    w_up,
    w_down,
):
    req_count = lax.axis_size("req")
    exp_count = lax.axis_size("exp")
    column = lax.axis_index("exp")
    rows_dev, heads_dev, head_size = queries.shape
    slots = keys.shape[1]
    kv_heads = keys.shape[2]
    group_rows, col_width = resid.shape
    full_width = norm_gain.shape[0]
    capacity = 2 * rows_dev
    expert_total = req_count * exp_count
    grouped_result = queries.reshape(rows_dev, kv_heads, heads_dev // kv_heads, head_size)
    logits = jnp.einsum(
        "rgjd,rcgd->rgjc", grouped_result, keys, preferred_element_type=jnp.float32
    ) * (1.0 / math.sqrt(head_size))
    visible = jnp.arange(slots, dtype=jnp.int32)[None, :] < lengths[:, None]
    logits = jnp.where(visible[:, None, None, :], logits, -1e30)
    peak = jnp.max(logits, axis=-1, keepdims=True)
    raised = jnp.exp(logits - peak)
    soft_weights = (raised / jnp.sum(raised, axis=-1, keepdims=True)).astype(jnp.bfloat16)
    attended = jnp.einsum(
        "rgjc,rcgd->rgjd", soft_weights, values, preferred_element_type=jnp.float32
    )
    attended = attended.reshape(rows_dev, heads_dev * head_size).astype(jnp.bfloat16)
    projected = jnp.dot(
        lax.all_gather(attended, "exp", axis=0, tiled=True),
        out_weight,
        preferred_element_type=jnp.float32,
    )
    projected = lax.psum(projected, "head")
    hidden = resid.astype(jnp.float32) + projected
    squares = lax.psum(jnp.sum(hidden * hidden, axis=1), "exp")
    inverse = lax.rsqrt(squares / full_width + 1e-06)
    gain_cols = lax.dynamic_slice_in_dim(norm_gain, column * col_width, col_width)
    normed_cols = (hidden * inverse[:, None] * gain_cols[None, :]).astype(jnp.bfloat16)
    matched = expert_ids[:, :, None] == jnp.arange(expert_total, dtype=jnp.int32)[None, None, :]
    chosen = jnp.any(matched, axis=1)
    weighting = jnp.sum(jnp.where(matched, route_weights[:, :, None], 0.0), axis=1)
    position = jnp.cumsum(chosen.astype(jnp.int32), axis=0) - 1
    selector = (
        position.T[:, None, :] == jnp.arange(capacity, dtype=jnp.int32)[None, :, None]
    ) & chosen.T[:, None, :]
    spread = jnp.where(selector, weighting.T[:, None, :], 0.0)
    outgoing = jnp.einsum(
        "ecg,gd->ecd",
        selector.astype(jnp.bfloat16),
        normed_cols,
        preferred_element_type=jnp.float32,
    ).astype(jnp.bfloat16)
    arrived = lax.all_to_all(outgoing, ("req", "exp"), split_axis=0, concat_axis=0, tiled=True)
    items = arrived.shape[1]
    rows = arrived.reshape(req_count, exp_count, items, col_width).transpose(0, 2, 1, 3)
    rows = rows.reshape(req_count, items, exp_count * col_width)
    gate_act = jnp.einsum("snd,df->snf", rows, w_gate[0], preferred_element_type=jnp.float32)
    up_act = jnp.einsum("snd,df->snf", rows, w_up[0], preferred_element_type=jnp.float32)
    activated = (jax.nn.silu(gate_act) * up_act).astype(jnp.bfloat16)
    expert_out = jnp.einsum("snf,fd->snd", activated, w_down[0], preferred_element_type=jnp.float32)
    expert_out = lax.psum(expert_out, "head")
    pieces = expert_out.reshape(req_count, items, exp_count, col_width).transpose(0, 2, 1, 3)
    pieces = pieces.reshape(req_count * exp_count, items, col_width)
    returned = lax.all_to_all(pieces, ("req", "exp"), split_axis=0, concat_axis=0, tiled=True)
    mixture = jnp.einsum("ecg,ecd->gd", spread, returned, precision=lax.Precision.HIGHEST)
    return (hidden + mixture).astype(jnp.bfloat16)


def solution(mesh):
    in_specs = (
        P(("req", "exp"), "head", None),
        P(("req", "exp"), None, "head", None),
        P(("req", "exp"), None, "head", None),
        P(("req", "exp")),
        P("head", "exp"),
        P("req", "exp"),
        P(),
        P("req", None),
        P("req", None),
        P(("req", "exp"), None, "head"),
        P(("req", "exp"), None, "head"),
        P(("req", "exp"), "head", None),
    )
    out_specs = P("req", "exp")
    return jax.shard_map(local, mesh=mesh, in_specs=in_specs, out_specs=out_specs, check_vma=False)
```

profile of v0, /device:TPU:0, one launch (start us, length us, event | category | flops | bytes accessed | tf_op | source)
XLA Modules:
  0.0 127.2 jit_solution(6337636310465268059)
XLA Ops:
  6.5 0.0 copy-start
  6.5 0.0 all-reduce.3.cloned.1.call-start
  6.5 0.9 iota_compare_fusion.2
  7.4 1.7 %fusion.9 = f32[4,2,16,512]{3,2,1,0:T(8,128)S(1)} fusion(bf16[4,2,16,128]{3,2,1,0:T(8,128)(2,1)} %bitcast.52, bf16[4,512,2,128]{3,2,1,0:T(2,128)(2,1)} %param.13, pred[4,512]{1,0:T(4,128)(4,1)S(1)} %iota_compare_fusion.2), kind=kOutput, calls=%fused_computation.11 | convolution fusion | flops 16908288 | bytes 1345536 | tf_op jit(solution)/shard_map/rgjd,rcgd->rgjc/dot_general | solution.py:33
  9.1 0.2 fusion.44
  9.3 1.5 %convolution_convert_fusion.1 = bf16[4,2,16,128]{3,2,1,0:T(8,128)(2,1)S(1)} fusion(bf16[4,512,2,128]{3,2,1,0:T(2,128)(2,1)} %param.14, f32[4,2,16]{2,1,0:T(2,128)S(1)} %fusion.44, f32[4,2,16,512]{3,2,1,0:T(8,128)S(1)} %fusion.9), kind=kOutput, calls=%fused_computation.16 | convolution fusion | flops 16990848 | bytes 1344000 | tf_op jit(solution)/shard_map/rgjc,rcgd->rgjd/dot_general | solution.py:41
  10.9 9.9 %all-gather = bf16[4,4,4096]{2,1,0:T(4,128)(2,1)S(1)} all-gather(bf16[1,4,4096]{2,1,0:T(4,128)(2,1)S(1)} %reshape.45), channel_id=1, replica_groups=mesh['req'=4,'head'=2,'exp'=4] {'exp'}, dimensions={0}, use_global_device_ids=true | all-gather | bytes 163840 | tf_op jit(solution)/shard_map/all_gather | solution.py:46
  20.9 0.0 copy-start.3
  20.9 0.0 copy-start.2
  20.9 5.2 %fusion.45 = f32[16,1024]{1,0:T(8,128)} fusion(bf16[16,4096]{1,0:T(8,128)(2,1)S(1)} %reshape.46, bf16[4096,1024]{1,0:T(8,128)(2,1)} %param.16), kind=kOutput, calls=%fused_computation.52 | convolution fusion | flops 134217728 | bytes 8585216 | tf_op jit(solution)/shard_map/dot_general | solution.py:45
  26.1 0.0 all-reduce.3.cloned.1.call-update
  26.1 0.0 all-reduce.5.cloned.1.call-start
  26.2 0.0 copy-done.3
  26.2 0.1 copy.19
  26.4 0.1 copy.20
  26.5 0.1 copy.22
  26.6 17.7 %all-reduce.3.cloned.1.call-done = f32[16,1024]{1,0:T(8,128)} async-done(((f32[16,1024]{1,0:T(8,128)}), f32[16,1024]{1,0:T(8,128)}) %all-reduce.3.cloned.1.call-update) | async-done | bytes 65552 | tf_op jit(solution)/shard_map/psum | solution.py:50
  44.3 0.0 copy-done.2
  44.3 1.0 multiply_reduce_fusion
  45.3 0.7 dynamic_slice.3
  46.0 10.1 %psum.22 = f32[16]{0:T(128)S(1)} all-reduce(f32[16]{0:T(128)S(1)} %multiply_reduce_fusion), channel_id=1, replica_groups=mesh['req'=4,'head'=2,'exp'=4] {'exp'}, use_global_device_ids=true, to_apply=%region_7.8 | all-reduce | flops 16 | bytes 128 | tf_op jit(solution)/shard_map/psum | solution.py:52
  56.1 1.1 convolution_convert_fusion
  57.2 13.0 %all_to_all.10 = bf16[16,8,1024]{2,1,0:T(8,128)(2,1)S(1)} all-to-all(bf16[16,8,1024]{2,1,0:T(8,128)(2,1)S(1)} %convolution_convert_fusion), channel_id=1, replica_groups=mesh['req'=4,'head'=2,'exp'=4] {'req','exp'}, dimensions={0} | all-to-all | bytes 524288 | tf_op jit(solution)/shard_map/all_to_all | solution.py:70
  70.2 2.4 %fusion.5 = f32[4,8,384]{2,1,0:T(8,128)S(1)} fusion(bf16[4,8,4096]{2,1,0:T(8,128)(2,1)S(1)} %bitcast.48, bf16[1,4096,384]{2,1,0:T(8,128)(2,1)} %param.21), kind=kOutput, calls=%fused_computation.5 | convolution fusion | flops 100663296 | bytes 3457024 | tf_op jit(solution)/shard_map/snd,df->snf/dot_general | solution.py:74
  72.7 0.0 copy-done
  72.7 4.1 %fusion.1 = f32[4,8,4096]{2,1,0:T(8,128)} fusion(bf16[1,384,4096]{2,1,0:T(8,128)(2,1)S(1)} %copy-done, bf16[4,8,4096]{2,1,0:T(8,128)(2,1)S(1)} %bitcast.49, bf16[1,4096,384]{2,1,0:T(8,128)(2,1)} %param.22, f32[4,8,384]{2,1,0:T(8,128)S(1)} %fusion.5), kind=kOutput, calls=%fused_computation.1 | convolution fusion | flops 201400320 | bytes 7127040 | tf_op jit(solution)/shard_map/snf,fd->snd/dot_general | solution.py:77
  76.8 0.0 copy-start.4
  76.8 0.0 copy-start.1
  76.8 0.0 all-reduce.5.cloned.1.call-update
  76.8 16.7 %all-reduce.5.cloned.1.call-done = f32[4,8,4096]{2,1,0:T(8,128)} async-done(((f32[4,8,4096]{2,1,0:T(8,128)}), f32[4,8,4096]{2,1,0:T(8,128)}) %all-reduce.5.cloned.1.call-update) | async-done | bytes 524304 | tf_op jit(solution)/shard_map/psum | solution.py:78
  93.4 1.1 fusion.43
  94.6 0.8 pad_maximum_fusion
  95.4 6.9 %all-to-all-start.1 = ((f32[16,8,1024]{2,1,0:T(8,128)}), f32[16,8,1024]{2,1,0:T(8,128)}, u32[]{:S(2)}, u32[]{:S(2)}) async-start(f32[16,8,1024]{2,1,0:T(8,128)} %bitcast.50), calls=%async_computation.1 | async-start | bytes 1048576 | tf_op jit(solution)/shard_map/all_to_all | solution.py:81
  102.3 0.0 copy-done.4
  102.3 0.1 copy.21
  102.4 15.4 %all-to-all-done.1 = f32[16,8,1024]{2,1,0:T(8,128)} async-done(((f32[16,8,1024]{2,1,0:T(8,128)}), f32[16,8,1024]{2,1,0:T(8,128)}, u32[]{:S(2)}, u32[]{:S(2)}) %all-to-all-start.1) | async-done | bytes 524320 | tf_op jit(solution)/shard_map/all_to_all | solution.py:81
  117.9 0.0 copy-done.1
  117.9 2.5 %fusion.14 = bf16[16,1024]{1,0:T(8,128)(2,1)} fusion(f32[16,8,1024]{2,1,0:T(8,128)} %all-to-all-done.1, f32[16,16]{0,1:T(8,128)S(1)} %copy.21, f32[16,1024]{1,0:T(8,128)S(1)} %copy-done.1, bf16[16,1024]{1,0:T(8,128)(2,1)S(1)} %copy-done.2, s32[16,16]{0,1:T(8,128)S(1)} %add_bitcast_fusion, pred[16,16]{0,1:T(8,128)(4,1)S(1)} %copy.20), kind=kOutput, calls=%fused_computation.15 | convolution fusion | flops 25237504 | bytes 657664 | tf_op jit(solution)/shard_map/ecg,ecd->gd/dot_general | solution.py:82
  (9 shorter events, 0.2 us)
Async XLA Ops:
  6.5 66.1 %copy-start = (bf16[1,384,4096]{2,1,0:T(8,128)(2,1)S(1)}, bf16[1,384,4096]{2,1,0:T(8,128)(2,1)}, u32[]{:S(2)}) copy-start(bf16[1,384,4096]{2,1,0:T(8,128)(2,1)} %param.23) | copy-start | bytes 9437188
  6.5 37.8 %all-reduce.3.cloned.1.call-start = ((), (), s32[]{:S(2)}) async-start(), calls=%async_computation.2 | async-start | bytes 131072 | tf_op jit(solution)/shard_map/psum | solution.py:50
  20.9 5.3 %copy-start.3 = (s32[16,8]{0,1:T(8,128)S(1)}, s32[16,8]{0,1:T(8,128)}, u32[]{:S(2)}) copy-start(s32[16,8]{0,1:T(8,128)} %param.19) | copy-start | bytes 1540
  20.9 23.4 %copy-start.2 = (bf16[16,1024]{1,0:T(8,128)(2,1)S(1)}, bf16[16,1024]{1,0:T(8,128)(2,1)}, u32[]{:S(2)}) copy-start(bf16[16,1024]{1,0:T(8,128)(2,1)} %param.17) | copy-start | bytes 98308
  26.1 67.3 %all-reduce.5.cloned.1.call-start = ((), (), s32[]{:S(2)}) async-start(), calls=%async_computation.3 | async-start | bytes 1048576 | tf_op jit(solution)/shard_map/psum | solution.py:78
  76.8 25.6 %copy-start.4 = (f32[16,8]{0,1:T(8,128)S(1)}, f32[16,8]{0,1:T(8,128)}, u32[]{:S(2)}) copy-start(f32[16,8]{0,1:T(8,128)} %param.20) | copy-start | bytes 1540
  76.8 41.1 %copy-start.1 = (f32[16,1024]{1,0:T(8,128)S(1)}, f32[16,1024]{1,0:T(8,128)}, u32[]{:S(2)}) copy-start(f32[16,1024]{1,0:T(8,128)} %all-reduce.3.cloned.1.call-done) | copy-start | bytes 196612
  95.4 22.4 %all-to-all-start.1 = ((f32[16,8,1024]{2,1,0:T(8,128)}), f32[16,8,1024]{2,1,0:T(8,128)}, u32[]{:S(2)}, u32[]{:S(2)}) async-start(f32[16,8,1024]{2,1,0:T(8,128)} %bitcast.50), calls=%async_computation.1 | async-start | bytes 1048576 | tf_op jit(solution)/shard_map/all_to_all | solution.py:81
Sparse Core Ops, SparseCore 0:
  26.3 17.9 all-reduce.2
  76.9 16.4 all-reduce.4
where the time goes:
time: 128 us; the launch traced here: 127 us
  waiting for transfers between devices  49.9 us (39%)
  blocking collectives  33.1 us (26%)
  matrix products  18.6 us (15%)
  between operations  13.5 us (11%)
  starting transfers between devices  6.92 us (5%)
  other arithmetic  3 us (2%)
  local copies, waits for them, and re-layouts  2.23 us (2%)
    psum x1, waiting for transfers between devices, local(): projected = lax.psum(projected, 'head')  17.7 us
    psum x1, waiting for transfers between devices, local(): expert_out = lax.psum(expert_out, 'head')  16.7 us
    all_to_all x1, waiting for transfers between devices, local(): lax.all_to_all(pieces, ('req', 'exp'), split_axis=0, concat_axis=0, tiled...  15.4 us
    all_to_all x1, blocking collectives, local(): lax.all_to_all(outgoing, ('req', 'exp'), split_axis=0, concat_axis=0, til...  13 us
    psum x1, blocking collectives, local(): squares = lax.psum(jnp.sum(hidden * hidden, axis=1), 'exp')  10.1 us
    all_gather x1, blocking collectives, local(): lax.all_gather(attended, 'exp', axis=0, tiled=True)  9.94 us
    all_to_all x1, starting transfers between devices, local(): lax.all_to_all(pieces, ('req', 'exp'), split_axis=0, concat_axis=0, tiled...  6.88 us
    dot_general x1, matrix products, local(): jnp.dot(lax.all_gather(attended, 'exp', axis=0, tiled=True), out_weight,...  5.21 us
  transfers between devices with their start and end apart: 3, of which 3 were waited for; matrix products, arithmetic and copies ran while one was open for 0% of the time, Pallas kernels for 0%

commit v1 on v0

--- a/solution.py
+++ b/solution.py
@@ -47,7 +47,7 @@
         out_weight,
         preferred_element_type=jnp.float32,
     )
-    projected = lax.psum(projected, "head")
+    projected = jnp.sum(lax.all_gather(projected, "head"), axis=0)
     hidden = resid.astype(jnp.float32) + projected
     squares = lax.psum(jnp.sum(hidden * hidden, axis=1), "exp")
     inverse = lax.rsqrt(squares / full_width + 1e-06)

time: 128 us -> 110 us (0.86)
  waiting for transfers between devices: 49.9 us -> 32.1 us
  blocking collectives: 33.1 us -> 35 us
  matrix products: 18.6 us -> 17.2 us
    psum x1 -> x0, waiting for transfers between devices: 17.7 us -> none  [local(): projected = lax.psum(projected, 'head')]
    all_gather x0 -> x1, blocking collectives: none -> 1.9 us  [local(): projected = jnp.sum(lax.all_gather(projected, 'head'), axis=0)]
  transfers between devices with their start and end apart: 3 -> 2, of which waited for: 3 -> 2; matrix products, arithmetic and copies ran while one was open for 0% -> 0% of each run, Pallas kernels for 0% -> 0%
where the time goes in v1:
time: 110 us
  blocking collectives  35 us (32%)
  waiting for transfers between devices  32.1 us (29%)
  matrix products  17.2 us (16%)
  between operations  13.5 us (12%)
  starting transfers between devices  6.88 us (6%)
  local copies, waits for them, and re-layouts  2.83 us (3%)
  other arithmetic  2.17 us (2%)
    psum x1, waiting for transfers between devices, local(): expert_out = lax.psum(expert_out, 'head')  16.6 us
    all_to_all x1, waiting for transfers between devices, local(): lax.all_to_all(pieces, ('req', 'exp'), split_axis=0, concat_axis=0, tiled...  15.4 us
    all_to_all x1, blocking collectives, local(): lax.all_to_all(outgoing, ('req', 'exp'), split_axis=0, concat_axis=0, til...  14.2 us
    all_gather x1, blocking collectives, local(): lax.all_gather(attended, 'exp', axis=0, tiled=True)  9.94 us
    psum x1, blocking collectives, local(): squares = lax.psum(jnp.sum(hidden * hidden, axis=1), 'exp')  8.95 us
    all_to_all x1, starting transfers between devices, local(): lax.all_to_all(pieces, ('req', 'exp'), split_axis=0, concat_axis=0, tiled...  6.88 us
    dot_general x1, matrix products, local(): jnp.dot(lax.all_gather(attended, 'exp', axis=0, tiled=True), out_weight,...  4.58 us
    dot_general x1, matrix products, local(): jnp.einsum('snf,fd->snd', activated, w_down[0], preferred_element_type=jn...  4.09 us
  transfers between devices with their start and end apart: 2, of which 2 were waited for; matrix products, arithmetic and copies ran while one was open for 0% of the time, Pallas kernels for 0%

profile of v1, /device:TPU:0, one launch (start us, length us, event | category | flops | bytes accessed | tf_op | source)
XLA Modules:
  0.0 109.6 jit_solution(2851812561246986492)
XLA Ops:
  6.5 0.0 copy-start
  6.5 0.0 all-reduce.2.cloned.1.call-start
  6.5 0.9 iota_compare_fusion.2
  7.4 1.7 %fusion.9 = f32[4,2,16,512]{3,2,1,0:T(8,128)S(1)} fusion(bf16[4,2,16,128]{3,2,1,0:T(8,128)(2,1)} %bitcast.54, bf16[4,512,2,128]{3,2,1,0:T(2,128)(2,1)} %param.13, pred[4,512]{1,0:T(4,128)(4,1)S(1)} %iota_compare_fusion.2), kind=kOutput, calls=%fused_computation.11 | convolution fusion | flops 16908288 | bytes 1345536 | tf_op jit(solution)/shard_map/rgjd,rcgd->rgjc/dot_general | solution.py:33
  9.1 0.2 fusion.44
  9.3 1.5 %convolution_convert_fusion.1 = bf16[4,2,16,128]{3,2,1,0:T(8,128)(2,1)S(1)} fusion(bf16[4,512,2,128]{3,2,1,0:T(2,128)(2,1)} %param.14, f32[4,2,16]{2,1,0:T(2,128)S(1)} %fusion.44, f32[4,2,16,512]{3,2,1,0:T(8,128)S(1)} %fusion.9), kind=kOutput, calls=%fused_computation.16 | convolution fusion | flops 16990848 | bytes 1344000 | tf_op jit(solution)/shard_map/rgjc,rcgd->rgjd/dot_general | solution.py:41
  10.9 9.9 %all-gather.1 = bf16[4,4,4096]{2,1,0:T(4,128)(2,1)S(1)} all-gather(bf16[1,4,4096]{2,1,0:T(4,128)(2,1)S(1)} %reshape.46), channel_id=1, replica_groups=mesh['req'=4,'head'=2,'exp'=4] {'exp'}, dimensions={0}, use_global_device_ids=true | all-gather | bytes 163840 | tf_op jit(solution)/shard_map/all_gather | solution.py:46
  20.9 0.0 copy-start.1
  20.9 0.0 copy-start.6
  20.9 4.6 %fusion.45 = f32[16,1024]{1,0:T(8,128)S(1)} fusion(bf16[16,4096]{1,0:T(8,128)(2,1)S(1)} %reshape.47, bf16[4096,1024]{1,0:T(8,128)(2,1)} %param.16), kind=kOutput, calls=%fused_computation.52 | convolution fusion | flops 134217728 | bytes 8585216 | tf_op jit(solution)/shard_map/dot_general | solution.py:45
  25.5 1.9 %all-gather = f32[32,1024]{1,0:T(8,128)S(1)} all-gather(f32[16,1024]{1,0:T(8,128)S(1)} %fusion.45), channel_id=2, replica_groups=mesh['req'=4,'head'=2,'exp'=4] {'head'}, dimensions={0}, use_global_device_ids=true | all-gather | bytes 196608 | tf_op jit(solution)/shard_map/all_gather | solution.py:50
  27.4 0.0 copy-done.1
  27.4 0.1 multiply_reduce_fusion
  27.5 9.0 %psum.14 = f32[16]{0:T(128)S(1)} all-reduce(f32[16]{0:T(128)S(1)} %multiply_reduce_fusion), channel_id=1, replica_groups=mesh['req'=4,'head'=2,'exp'=4] {'exp'}, use_global_device_ids=true, to_apply=%region_7.8 | all-reduce | flops 16 | bytes 128 | tf_op jit(solution)/shard_map/psum | solution.py:52
  36.5 0.0 copy-done.6
  36.5 0.1 copy.19
  36.7 0.0 copy-start.2
  36.7 0.1 copy.20
  36.8 0.0 copy-start.4
  36.8 0.6 copy-done.4
  37.4 0.1 copy.22
  37.5 0.7 dynamic_slice.3
  38.2 0.0 copy-done.2
  38.2 0.3 convolution_convert_fusion
  38.4 14.2 %all_to_all.10 = bf16[16,8,1024]{2,1,0:T(8,128)(2,1)S(1)} all-to-all(bf16[16,8,1024]{2,1,0:T(8,128)(2,1)S(1)} %convolution_convert_fusion), channel_id=1, replica_groups=mesh['req'=4,'head'=2,'exp'=4] {'req','exp'}, dimensions={0} | all-to-all | bytes 524288 | tf_op jit(solution)/shard_map/all_to_all | solution.py:70
  52.6 2.4 %fusion.5 = f32[4,8,384]{2,1,0:T(8,128)S(1)} fusion(bf16[4,8,4096]{2,1,0:T(8,128)(2,1)S(1)} %bitcast.49, bf16[1,4096,384]{2,1,0:T(8,128)(2,1)} %param.21), kind=kOutput, calls=%fused_computation.5 | convolution fusion | flops 100663296 | bytes 3457024 | tf_op jit(solution)/shard_map/snd,df->snf/dot_general | solution.py:74
  55.1 0.0 copy-done
  55.1 4.1 %fusion.1 = f32[4,8,4096]{2,1,0:T(8,128)} fusion(bf16[1,384,4096]{2,1,0:T(8,128)(2,1)S(1)} %copy-done, bf16[4,8,4096]{2,1,0:T(8,128)(2,1)S(1)} %bitcast.50, bf16[1,4096,384]{2,1,0:T(8,128)(2,1)} %param.22, f32[4,8,384]{2,1,0:T(8,128)S(1)} %fusion.5), kind=kOutput, calls=%fused_computation.1 | convolution fusion | flops 201400320 | bytes 7127040 | tf_op jit(solution)/shard_map/snf,fd->snd/dot_general | solution.py:77
  59.2 0.0 copy-start.7
  59.2 0.0 copy-start.8
  59.2 0.0 copy-start.3
  59.2 0.0 copy-start.5
  59.2 0.0 all-reduce.2.cloned.1.call-update
  59.2 16.6 %all-reduce.2.cloned.1.call-done = f32[4,8,4096]{2,1,0:T(8,128)} async-done(((f32[4,8,4096]{2,1,0:T(8,128)}), f32[4,8,4096]{2,1,0:T(8,128)}) %all-reduce.2.cloned.1.call-update) | async-done | bytes 524304 | tf_op jit(solution)/shard_map/psum | solution.py:78
  75.8 1.1 %fusion.43 = (f32[4,8,1024]{2,1,0:T(8,128)S(1)}, f32[4,8,1024]{2,1,0:T(8,128)S(1)}, f32[4,8,1024]{2,1,0:T(8,128)S(1)}, f32[4,8,1024]{2,1,0:T(8,128)S(1)}) fusion(f32[4,8,4096]{2,1,0:T(8,128)} %all-reduce.2.cloned.1.call-done), kind=kLoop, calls=%fused_computation.50 | loop fusion | bytes 1048576 | tf_op jit(solution)/shard_map/slice
  77.0 0.8 pad_maximum_fusion
  77.8 6.9 %all-to-all-start.1 = ((f32[16,8,1024]{2,1,0:T(8,128)}), f32[16,8,1024]{2,1,0:T(8,128)}, u32[]{:S(2)}, u32[]{:S(2)}) async-start(f32[16,8,1024]{2,1,0:T(8,128)} %bitcast.51), calls=%async_computation.1 | async-start | bytes 1048576 | tf_op jit(solution)/shard_map/all_to_all | solution.py:81
  84.7 0.0 copy-done.7
  84.7 0.0 copy-done.8
  84.7 0.1 copy.21
  84.8 15.4 %all-to-all-done.1 = f32[16,8,1024]{2,1,0:T(8,128)} async-done(((f32[16,8,1024]{2,1,0:T(8,128)}), f32[16,8,1024]{2,1,0:T(8,128)}, u32[]{:S(2)}, u32[]{:S(2)}) %all-to-all-start.1) | async-done | bytes 524320 | tf_op jit(solution)/shard_map/all_to_all | solution.py:81
  100.2 0.0 copy-done.3
  100.2 0.0 copy-done.5
  100.2 2.5 %fusion.14 = bf16[16,1024]{1,0:T(8,128)(2,1)} fusion(f32[16,8,1024]{2,1,0:T(8,128)} %all-to-all-done.1, f32[16,16]{0,1:T(8,128)S(1)} %copy.21, f32[16,1024]{1,0:T(8,128)S(1)} %reduce_sum.37, bf16[16,1024]{1,0:T(8,128)(2,1)S(1)} %copy-done.1, s32[16,16]{0,1:T(8,128)S(1)} %copy-done.3, pred[16,16]{0,1:T(8,128)(4,1)S(1)} %copy-done.5), kind=kOutput, calls=%fused_computation.15 | convolution fusion | flops 25237504 | bytes 657664 | tf_op jit(solution)/shard_map/ecg,ecd->gd/dot_general | solution.py:82
  (10 shorter events, 0.2 us)
Async XLA Ops:
  6.5 48.5 %copy-start = (bf16[1,384,4096]{2,1,0:T(8,128)(2,1)S(1)}, bf16[1,384,4096]{2,1,0:T(8,128)(2,1)}, u32[]{:S(2)}) copy-start(bf16[1,384,4096]{2,1,0:T(8,128)(2,1)} %param.23) | copy-start | bytes 9437188
  6.5 69.3 %all-reduce.2.cloned.1.call-start = ((), (), s32[]{:S(2)}) async-start(), calls=%async_computation.2 | async-start | bytes 1048576 | tf_op jit(solution)/shard_map/psum | solution.py:78
  20.9 6.5 %copy-start.1 = (bf16[16,1024]{1,0:T(8,128)(2,1)S(1)}, bf16[16,1024]{1,0:T(8,128)(2,1)}, u32[]{:S(2)}) copy-start(bf16[16,1024]{1,0:T(8,128)(2,1)} %param.17) | copy-start | bytes 98308
  20.9 15.6 %copy-start.6 = (s32[16,8]{0,1:T(8,128)S(1)}, s32[16,8]{0,1:T(8,128)}, u32[]{:S(2)}) copy-start(s32[16,8]{0,1:T(8,128)} %param.19) | copy-start | bytes 1540
  36.7 1.5 %copy-start.2 = (s32[16,16]{0,1:T(8,128)}, s32[16,16]{0,1:T(8,128)S(1)}, u32[]{:S(2)}) copy-start(s32[16,16]{0,1:T(8,128)S(1)} %add_bitcast_fusion) | copy-start | bytes 3076
  36.8 0.6 copy-start.4
  59.2 25.5 %copy-start.7 = (s32[16,8]{0,1:T(8,128)S(1)}, s32[16,8]{0,1:T(8,128)}, u32[]{:S(2)}) copy-start(s32[16,8]{0,1:T(8,128)} %param.19) | copy-start | bytes 1540
  59.2 25.6 %copy-start.8 = (f32[16,8]{0,1:T(8,128)S(1)}, f32[16,8]{0,1:T(8,128)}, u32[]{:S(2)}) copy-start(f32[16,8]{0,1:T(8,128)} %param.20) | copy-start | bytes 1540
  59.2 41.1 %copy-start.3 = (s32[16,16]{0,1:T(8,128)S(1)}, s32[16,16]{0,1:T(8,128)}, u32[]{:S(2)}) copy-start(s32[16,16]{0,1:T(8,128)} %copy-done.2) | copy-start | bytes 3076
  59.2 41.1 %copy-start.5 = (pred[16,16]{0,1:T(8,128)(4,1)S(1)}, pred[16,16]{0,1:T(8,128)(4,1)}, u32[]{:S(2)}) copy-start(pred[16,16]{0,1:T(8,128)(4,1)} %copy-done.4) | copy-start | bytes 772
  77.8 22.4 %all-to-all-start.1 = ((f32[16,8,1024]{2,1,0:T(8,128)}), f32[16,8,1024]{2,1,0:T(8,128)}, u32[]{:S(2)}, u32[]{:S(2)}) async-start(f32[16,8,1024]{2,1,0:T(8,128)} %bitcast.51), calls=%async_computation.1 | async-start | bytes 1048576 | tf_op jit(solution)/shard_map/all_to_all | solution.py:81
Sparse Core Ops, SparseCore 0:
  59.3 16.4 all-reduce.1
